TPU v7x, 32 devices: a whole 2x2x4 slice. The times are simulated.
32 devices in a mesh: groups: 2 (over x), ctx: 8 (over z, y), exp: 2 (over core).
Axes of the slice: x: 2, y: 2, z: 4, core: 2. Of those that a mesh axis runs over, the one named last changes fastest.
Arguments:
- x_in: bfloat16 [4096, 2048], P(('groups', 'ctx'), 'exp'), parts along dimension 0, may hold values from -6 to 6
- bc_in: bfloat16 [4096, 2, 512], P(('groups', 'ctx'), None, 'exp'), parts along dimension 0, may hold values from -6 to 6
- z_in: bfloat16 [4096, 2048], P(('groups', 'ctx'), 'exp'), parts along dimension 0, may hold values from -6 to 6
- time_step: float32 [4096, 32], P(('groups', 'ctx'), 'exp'), parts along dimension 0, may hold values from 0.002 to 0.02
- decay_log: float32 [4096, 32], P(('groups', 'ctx'), 'exp'), parts along dimension 0, may hold values from -1 to 0
- conv_inner: bfloat16 [4, 2048], P(None, 'exp'), may hold values from -3 to 3
- conv_bc: bfloat16 [4, 2, 512], P(None, None, 'exp'), may hold values from -3 to 3
- skip_gain: float32 [32], P('exp'), may hold values from 0.5 to 1.5
- start_state: bfloat16 [64, 64, 128], P(('groups', 'exp')), parts along dimension 0, may hold values from -3 to 3
- norm_gain: bfloat16 [2048], P('exp'), may hold values from 0.099609375 to 1.8984375
- out_proj: bfloat16 [2048, 2688], P('exp', 'ctx'), may hold values from -0.125 to 0.125
- residual: bfloat16 [4096, 2688], P(('groups', 'ctx', 'exp')), parts along dimension 0, may hold values from -40 to 40
- moe_gain: bfloat16 [2688], replicated, may hold values from 0.099609375 to 1.8984375
- routes: int32 [4096, 6], P(('groups', 'ctx', 'exp')), parts along dimension 0, may hold values from 0 to 15, all different within a row; in each aligned block of 128 rows (0 to 127, 128 to 255, ...) at most 64 rows name the same one
- gate_weight: float32 [4096, 6], P(('groups', 'ctx', 'exp')), parts along dimension 0, may hold values from 0.1 to 0.4
- up_weight: bfloat16 [16, 2688, 928], P(('ctx', 'exp')), may hold values from -0.125 to 0.125
- down_weight: bfloat16 [16, 928, 2688], P(('ctx', 'exp')), may hold values from -0.1875 to 0.1875
Outputs:
- layer_out: bfloat16 [4096, 2688], P(('groups', 'ctx', 'exp')), parts along dimension 0
There are 2 independent parts, one for each index of `groups`. A program takes and returns all parts, laid end to end along the dimension named above; an argument that names none is the same for every part. Nothing has to cross between parts.
Inputs may be any that keep to these rules, and one draw needn't show every extreme that they name: `routes`: each row names 6 different experts; among the rows of one device (aligned blocks of 128 rows) no expert is named more than 64 times.
All inputs are finite; a program needn't handle non-finite values.
Results may differ from a plain program's by a relative error of at most 0.0056.
Values may be sent and summed in bfloat16 or wider, within the bound.
No kernel may reach another device: no remote copies, remote signals or barrier semaphores. Data moves between devices by JAX's collectives and lax.ppermute only.
A program may use at most 128 MiB of HBM per device.

v0:
```python
import jax
import jax.numpy as jnp
from jax import lax
from jax.sharding import PartitionSpec as P

HEAD_DIM = 64
STATE = 128
KERNEL = 4
EPS = 1e-05
HIGH = lax.Precision.HIGHEST


def from_behind(array, axis, by):
    count = lax.axis_size(axis)
    pairs = [(i, i + by) for i in range(count) if 0 <= i + by < count]
    return lax.ppermute(array, axis, pairs)


def carried_in(array, axis, combine, identity):
    count, index = (lax.axis_size(axis), lax.axis_index(axis))
    everything = jax.tree.map(lambda part: lax.all_gather(part, axis), array)
    start = jax.tree.map(
        lambda part, zero: jnp.broadcast_to(jnp.asarray(zero, part.dtype), part.shape),
        array,
        identity,
    )

    def hop(k, before):
        reached = k < index
        new = combine(before, jax.tree.map(lambda part: part[k], everything))
        return jax.tree.map(lambda a, b: jnp.where(reached, a, b), new, before)

    return lax.fori_loop(0, count, hop, start)


def causal_conv(sequence, previous, taps):
    length = sequence.shape[0]
    padded = jnp.concatenate([previous, sequence], 0).astype(jnp.float32)
    summed = jnp.zeros(sequence.shape, jnp.float32)
    for offset in range(taps.shape[0]):
        summed = summed + taps[offset].astype(jnp.float32) * padded[offset : offset + length]
    return jax.nn.silu(summed).astype(jnp.bfloat16)


def chain_pair(earlier, later):
    return (earlier[0] * later[0], later[0][..., None, None] * earlier[1] + later[1])


def per_device(
    x_in,
    bc_in,
    z_in,
    time_step,
    decay_log,
    conv_inner,
    conv_bc,
    skip_gain,
    start_state,
    norm_gain,
    out_proj,
    residual,
    moe_gain,
    routes,
    gate_weight,
    up_weight,
    down_weight,
):
    block_len = x_in.shape[0]
    local_heads = time_step.shape[1]
    local_groups = bc_in.shape[2] // STATE
    per_group = local_heads // local_groups
    rim_rows = KERNEL - 1
    prev_inner, prev_bc = from_behind(
        (x_in[block_len - rim_rows :], bc_in[block_len - rim_rows :]), "ctx", 1
    )
    inner_act = causal_conv(x_in, prev_inner, conv_inner)
    bc_act = causal_conv(bc_in, prev_bc, conv_bc)
    values = inner_act.astype(jnp.float32).reshape(block_len, local_groups, per_group, HEAD_DIM)
    b_rows = bc_act[:, 0].astype(jnp.float32).reshape(block_len, local_groups, STATE)
    c_rows = bc_act[:, 1].astype(jnp.float32).reshape(block_len, local_groups, STATE)
    log_steps = decay_log.reshape(block_len, local_groups, per_group)
    step_sizes = time_step.reshape(block_len, local_groups, per_group)
    cumulative = jnp.cumsum(log_steps, axis=0)
    block_log = cumulative[block_len - 1]
    to_end = jnp.exp(block_log[None] - cumulative) * step_sizes
    end_state = jnp.einsum("tgrp,tgn->grpn", to_end[..., None] * values, b_rows, precision=HIGH)
    block_decay = jnp.exp(block_log)
    prior_decay, prior_state = carried_in(
        (block_decay, end_state),
        "ctx",
        chain_pair,
        (jnp.ones_like(block_decay), jnp.zeros_like(end_state)),
    )
    entering = (
        prior_decay[..., None, None]
        * start_state.astype(jnp.float32).reshape(local_groups, per_group, HEAD_DIM, STATE)
        + prior_state
    )
    carried = jnp.exp(cumulative)[..., None] * jnp.einsum(
        "tgn,grpn->tgrp", c_rows, entering, precision=HIGH
    )
    scores = jnp.einsum("tgn,sgn->tsg", c_rows, b_rows, precision=HIGH)
    position = jnp.arange(block_len)
    causal = (position[:, None] >= position[None, :])[:, :, None, None]
    spread_log = cumulative[:, None] - cumulative[None, :]
    decay_table = jnp.where(causal, jnp.exp(jnp.where(causal, spread_log, 0.0)), 0.0)
    mix_table = decay_table * step_sizes[None] * scores[..., None]
    local_part = jnp.einsum("tsgr,sgrp->tgrp", mix_table, values, precision=HIGH)
    outputs = (
        carried + local_part + skip_gain.reshape(local_groups, per_group)[None, :, :, None] * values
    )
    gated = outputs.reshape(block_len, local_groups, -1) * jax.nn.silu(
        z_in.astype(jnp.float32).reshape(block_len, local_groups, -1)
    )
    mean_square = jnp.mean(gated * gated, axis=-1, keepdims=True)
    normed = (
        (
            gated
            * lax.rsqrt(mean_square + EPS)
            * norm_gain.astype(jnp.float32).reshape(local_groups, -1)
        )
        .reshape(block_len, -1)
        .astype(jnp.bfloat16)
    )
    partial_out = jnp.dot(
        normed,
        lax.all_gather(out_proj, "ctx", axis=1, tiled=True),
        preferred_element_type=jnp.float32,
    )
    mixed = lax.psum_scatter(partial_out, "exp", scatter_dimension=0, tiled=True)
    hidden_f = (residual.astype(jnp.float32) + mixed).astype(jnp.bfloat16).astype(jnp.float32)
    expert_in = (
        hidden_f
        * lax.rsqrt(jnp.mean(hidden_f * hidden_f, axis=-1, keepdims=True) + EPS)
        * moe_gain.astype(jnp.float32)
    ).astype(jnp.bfloat16)
    tok_rows = routes.shape[0]
    top_count = routes.shape[1]
    model_width = expert_in.shape[1]
    ctx_count = lax.axis_size("ctx")
    exp_count = lax.axis_size("exp")
    experts = ctx_count * exp_count * up_weight.shape[0]
    capacity = max(2, 4 * tok_rows * top_count // (3 * experts))
    flat_ids = routes.reshape(-1)
    one_hot = (flat_ids[:, None] == jnp.arange(experts, dtype=jnp.int32)[None, :]).astype(jnp.int32)
    ranks = jnp.cumsum(one_hot, axis=0) - 1
    slots = jnp.sum(one_hot * ranks, axis=1)
    source_rows = jnp.repeat(jnp.arange(tok_rows, dtype=jnp.int32), top_count)
    send_buffer = (
        jnp.zeros((experts, capacity, model_width), jnp.bfloat16)
        .at[flat_ids, slots]
        .set(expert_in[source_rows])
    )
    arrived = lax.all_to_all(send_buffer, ("ctx", "exp"), split_axis=0, concat_axis=0, tiled=True)
    leading = arrived.shape[:-1]
    flat_rows = arrived.reshape(-1, arrived.shape[-1])
    inner = jnp.dot(flat_rows, up_weight[0], preferred_element_type=jnp.float32)
    inner = jnp.square(jax.nn.relu(inner)).astype(jnp.bfloat16)
    layer_answer = jnp.dot(inner, down_weight[0], preferred_element_type=jnp.float32).astype(
        jnp.bfloat16
    )
    finished = layer_answer.reshape(leading + (arrived.shape[-1],))
    returned = lax.all_to_all(finished, ("ctx", "exp"), split_axis=0, concat_axis=0, tiled=True)
    gathered = returned[flat_ids, slots].reshape(tok_rows, top_count, model_width)
    combined = jnp.sum(gate_weight[..., None] * gathered.astype(jnp.float32), axis=1)
    return (hidden_f + combined).astype(jnp.bfloat16)


def solution(mesh):
    in_specs = (
        P(("groups", "ctx"), "exp"),
        P(("groups", "ctx"), None, "exp"),
        P(("groups", "ctx"), "exp"),
        P(("groups", "ctx"), "exp"),
        P(("groups", "ctx"), "exp"),
        P(None, "exp"),
        P(None, None, "exp"),
        P("exp"),
        P(("groups", "exp"), None, None),
        P("exp"),
        P("exp", "ctx"),
        P(("groups", "ctx", "exp"), None),
        P(),
        P(("groups", "ctx", "exp"), None),
        P(("groups", "ctx", "exp"), None),
        P(("ctx", "exp"), None, None),
        P(("ctx", "exp"), None, None),
    )
    out_specs = P(("groups", "ctx", "exp"), None)
    return jax.shard_map(
        per_device, mesh=mesh, in_specs=in_specs, out_specs=out_specs, check_vma=False
    )
```

profile of v0, /device:TPU:13, one launch (start us, length us, event | category | flops | bytes accessed | tf_op | source)
XLA Modules:
  0.0 684.6 jit_solution(16131043887685088930)
XLA Ops:
  6.5 0.7 slice.88
  7.5 3.1 collective-permute-start.1
  10.6 0.7 slice.79
  11.4 3.1 collective-permute-start
  14.5 0.9 slice_convert_fusion.3
  15.4 1.2 reduce-window.14
  17.0 0.6 slice_bitcast_fusion
  17.6 0.9 copy.94
  18.8 0.7 bitcast_convert_fusion.3
  19.5 1.1 copy.98
  20.9 0.8 multiply_convert_fusion.4
  21.7 0.7 fusion.53
  22.6 0.6 multiply_convert_fusion.2
  23.4 1.5 fusion.29
  25.0 0.7 all-gather.4.cloned.1.call-update
  26.2 0.6 convert_element_type.82
  26.8 10.8 %all_gather.13 = f32[8,2,8]{2,1,0:T(2,128)S(1)} all-gather(f32[1,2,8]{2,1,0:T(2,128)S(1)} %copy-done.10), channel_id=1, replica_groups=mesh['groups'=2,'ctx'=8,'exp'=2] {'ctx'}, dimensions={0}, use_global_device_ids=true | all-gather | bytes 576 | tf_op jit(solution)/shard_map/all_gather | solution.py:21
  37.6 1.2 convolution_bitcast_fusion.1
  38.8 1.0 copy.105
  39.8 5.4 fusion.23
  45.2 51.4 %all-gather.6.cloned.1.call-done = f32[16,8,64,128]{3,2,1,0:T(8,128)} async-done(((f32[2,8,64,128]{3,2,1,0:T(8,128)}), f32[16,8,64,128]{3,2,1,0:T(8,128)}) %all-gather.6.cloned.1.call-update) | async-done | bytes 4194320 | tf_op jit(solution)/shard_map/all_gather | solution.py:21
  96.6 9.7 %while.16 = (s32[]{:T(128)}, f32[2,8]{1,0:T(2,128)S(1)}, f32[2,8,64,128]{3,2,1,0:T(8,128)S(1)}, s32[]{:T(128)}, f32[8,2,8]{2,1,0:T(2,128)S(1)}, /*index=5*/f32[8,2,8,64,128]{4,3,2,1,0:T(8,128)}, s32[]{:T(128)}, s32[]{:T(128)}) while((s32[]{:T(128)}, f32[2,8]{1,0:T(2,128)S(1)}, f32[2,8,64,128]{3,2,1,0:T(8,128)S(1)}, s32[]{:T(128)}, ...), condition=%wide.region_3.4_spmd.clone, body=%wide.region_2.3_spmd.clone.sunk | while | flops 524340 | bytes 1573299 | solution.py:33
  96.6 1.2 fusion.72
  97.8 1.2 fusion.72
  99.0 1.2 fusion.72
  100.2 1.2 fusion.72
  101.4 1.2 fusion.72
  102.7 1.2 fusion.72
  103.9 1.2 fusion.72
  105.1 1.2 fusion.72
  106.3 3.2 multiply_reduce_fusion.1
  110.2 1.6 copy.106
  111.8 74.2 %all-gather.4.cloned.1.call-done = bf16[1024,2688]{0,1:T(8,128)(2,1)} async-done(((bf16[1024,336]{0,1:T(8,128)(2,1)}), bf16[1024,2688]{0,1:T(8,128)(2,1)}) %all-gather.4.cloned.1.call-update) | async-done | bytes 5505040 | tf_op jit(solution)/shard_map/all_gather | solution.py:127
  186.0 6.1 fusion.33
  192.9 1.7 reduce-window.16
  195.0 9.6 %reduce-scatter.2.cloned.1.call-done = f32[128,2688]{1,0:T(8,128)} async-done(((f32[256,2688]{1,0:T(8,128)}), f32[128,2688]{1,0:T(8,128)}) %reduce-scatter.2.cloned.1.call-update) | async-done | bytes 1376272 | tf_op jit(solution)/shard_map/reduce_scatter | solution.py:130
  204.6 1.6 fusion.19
  206.5 4.9 gather_fusion
  211.4 3.0 broadcast_in_dim.27
  214.3 158.3 %scatter_fusion = bf16[16,64,2688]{2,1,0:T(8,128)(2,1)} fusion(bf16[16,64,2688]{2,1,0:T(8,128)(2,1)} %broadcast_in_dim.27, s32[768]{0:T(1024)S(1)} %get-tuple-element.151, bf16[768,2688]{1,0:T(8,128)(2,1)} %gather_fusion), kind=kCustom, calls=%fused_computation.2 | custom fusion | bytes 12392448 | tf_op jit(solution)/shard_map/scatter | solution.py:152
  372.6 126.7 %all_to_all.10 = bf16[16,64,2688]{2,1,0:T(8,128)(2,1)} all-to-all(bf16[16,64,2688]{2,1,0:T(8,128)(2,1)} %scatter_fusion), channel_id=1, replica_groups=mesh['groups'=2,'ctx'=8,'exp'=2] {'ctx','exp'}, dimensions={0} | all-to-all | bytes 11010048 | tf_op jit(solution)/shard_map/all_to_all | solution.py:154
  499.3 18.8 %convolution_convert_fusion = bf16[1024,2688]{1,0:T(8,128)(2,1)} fusion(bf16[1,928,2688]{2,1,0:T(8,128)(2,1)} %param.35, bf16[1024,2688]{1,0:T(8,128)(2,1)} %bitcast.116, bf16[1,2688,928]{1,2,0:T(8,128)(2,1)} %param.34), kind=kOutput, calls=%fused_computation.8 | convolution fusion | flops 10222927872 | bytes 20987904 | tf_op jit(solution)/shard_map/dot_general | solution.py:159
  518.1 5.6 all-to-all-start.1
  523.9 120.5 %all-to-all-done.1 = bf16[16,64,2688]{2,1,0:T(8,128)(2,1)} async-done(((bf16[16,64,2688]{2,1,0:T(8,128)(2,1)}), bf16[16,64,2688]{2,1,0:T(8,128)(2,1)}, u32[]{:S(2)}, u32[]{:S(2)}) %all-to-all-start.1) | async-done | bytes 5505056 | tf_op jit(solution)/shard_map/all_to_all | solution.py:163
  644.3 16.7 %gather_fusion.1 = bf16[768,2688]{1,0:T(8,128)(2,1)} fusion(bf16[16,64,2688]{2,1,0:T(8,128)(2,1)} %all-to-all-done.1, s32[768]{0:T(1024)S(1)} %get-tuple-element.150), kind=kCustom, calls=%fused_computation.1 | custom fusion | bytes 8263680 | tf_op jit(solution)/shard_map/gather | solution.py:164
  661.0 7.9 %reshape.218 = f32[128,6,2688]{2,1,0:T(8,128)} reshape(bf16[768,2688]{1,0:T(8,128)(2,1)} %gather_fusion.1) | data formatting | bytes 12386304 | tf_op jit(solution)/shard_map/convert_element_type | solution.py:165
  668.9 8.1 %multiply_reduce_fusion = f32[128,2688]{1,0:T(8,128)S(1)} fusion(f32[128,6,2688]{2,1,0:T(8,128)} %reshape.218, f32[128,6]{1,0:T(8,128)S(1)} %copy.109), kind=kLoop, calls=%fused_computation.7 | loop fusion | flops 3784704 | bytes 9636864 | tf_op jit(solution)/shard_map/reduce_sum | solution.py:165
  677.1 1.0 fusion.22
  (87 shorter events, 4.6 us)
Async XLA Ops:
  6.5 8.8 %copy-start = (f32[256,16]{0,1:T(8,128)S(1)}, f32[256,16]{0,1:T(8,128)}, u32[]{:S(2)}) copy-start(f32[256,16]{0,1:T(8,128)} %param.23) | copy-start | bytes 49156
  6.5 15.8 %copy-start.3 = (bf16[256,1024]{1,0:T(8,128)(2,1)S(1)}, bf16[256,1024]{1,0:T(8,128)(2,1)}, u32[]{:S(2)}) copy-start(bf16[256,1024]{1,0:T(8,128)(2,1)} %param.19) | copy-start | bytes 1572868
  6.5 90.0 %all-gather.6.cloned.1.call-start = ((), (), s32[]{:S(2)}) async-start(), calls=%async_computation.5 | async-start | bytes 4718592 | tf_op jit(solution)/shard_map/all_gather | solution.py:21
  7.5 13.2 %collective-permute-start.1 = (bf16[3,2,256]{0,2,1:T(8,128)(2,1)S(1)}, bf16[3,2,256]{0,2,1:T(8,128)(2,1)S(1)}, u32[]{:S(2)}, u32[]{:S(2)}) collective-permute-start(bf16[3,2,256]{0,2,1:T(8,128)(2,1)S(1)} %copy.97), channel_id=1, source_target_pairs={{0,2},{2,4},{4,6},{6,8},{8,10},{10,12},{12,14},{1,3},{3,5},{5,7},{... | collective-permute-start | bytes 9224 | tf_op jit(solution)/shard_map/ppermute | solution.py:16
  11.4 11.0 %collective-permute-start = (bf16[3,1024]{1,0:T(4,128)(2,1)S(1)}, bf16[3,1024]{1,0:T(4,128)(2,1)S(1)}, u32[]{:S(2)}, u32[]{:S(2)}) collective-permute-start(bf16[3,1024]{1,0:T(4,128)(2,1)S(1)} %slice.79), channel_id=1, source_target_pairs={{0,2},{2,4},{4,6},{6,8},{8,10},{10,12},{12,14},{1,3},{3,5},{5,7},{... | collective-permute-start | bytes 18440 | tf_op jit(solution)/shard_map/ppermute | solution.py:16
  22.5 3.4 copy-start.4
  22.5 3.6 copy-start.14
  22.5 3.7 copy-start.12
  22.6 4.3 copy-start.10
  23.4 16.4 %copy-start.6 = (f32[256,16]{0,1:T(8,128)S(1)}, f32[256,16]{0,1:T(8,128)}, u32[]{:S(2)}) copy-start(f32[256,16]{0,1:T(8,128)} %param.22) | copy-start | bytes 49156
  24.9 161.1 %all-gather.4.cloned.1.call-start = ((), (), s32[]{:S(2)}) async-start(), calls=%async_computation.3 | async-start | bytes 6193152 | tf_op jit(solution)/shard_map/all_gather | solution.py:127
  25.7 178.9 %reduce-scatter.2.cloned.1.call-start = ((), (), s32[]{:S(2)}) async-start(), calls=%async_computation.4 | async-start | bytes 4128768 | tf_op jit(solution)/shard_map/reduce_scatter | solution.py:130
  45.2 61.1 %copy-start.5 = (bf16[256,1,256]{0,2,1:T(8,128)(2,1)S(1)}, bf16[256,1,256]{0,2,1:T(8,128)(2,1)}, u32[]{:S(2)}) copy-start(bf16[256,1,256]{0,2,1:T(8,128)(2,1)} %get-tuple-element.172) | copy-start | bytes 393220
  45.2 61.1 %copy-start.13 = (bf16[16,64,128]{2,1,0:T(8,128)(2,1)S(1)}, bf16[16,64,128]{2,1,0:T(8,128)(2,1)}, u32[]{:S(2)}) copy-start(bf16[16,64,128]{2,1,0:T(8,128)(2,1)} %param.27) | copy-start | bytes 786436
  109.5 76.5 %copy-start.11 = (f32[1024]{0:T(1024)S(1)}, f32[1024]{0:T(1024)}, u32[]{:S(2)}) copy-start(f32[1024]{0:T(1024)} %convert_element_type.82) | copy-start | bytes 12292
  186.0 6.1 copy-start.8
  186.0 6.7 copy-start.7
  186.0 18.6 %copy-start.2 = (bf16[128,2688]{1,0:T(8,128)(2,1)S(1)}, bf16[128,2688]{1,0:T(8,128)(2,1)}, u32[]{:S(2)}) copy-start(bf16[128,2688]{1,0:T(8,128)(2,1)} %param.30) | copy-start | bytes 2064388
  518.1 5.6 copy-start.9
  518.1 126.2 %all-to-all-start.1 = ((bf16[16,64,2688]{2,1,0:T(8,128)(2,1)}), bf16[16,64,2688]{2,1,0:T(8,128)(2,1)}, u32[]{:S(2)}, u32[]{:S(2)}) async-start(bf16[16,64,2688]{2,1,0:T(8,128)(2,1)} %bitcast.115), calls=%async_computation.2 | async-start | bytes 11010048 | tf_op jit(solution)/shard_map/all_to_all | solution.py:163
  668.9 9.1 %copy-start.1 = (f32[256,16]{0,1:T(8,128)S(1)}, f32[256,16]{0,1:T(8,128)}, u32[]{:S(2)}) copy-start(f32[256,16]{0,1:T(8,128)} %param.23) | copy-start | bytes 49156
Sparse Core Ops, SparseCore 0:
  25.0 71.4 all-gather.5
  98.7 87.2 all-gather.3
  192.2 12.3 reduce-scatter.1
where the time goes:
time: 688 us; the launch traced here: 685 us
  waiting for transfers between devices  256 us (37%)
  local copies, waits for them, and re-layouts  201 us (29%)
  blocking collectives  137 us (20%)
  matrix products  36.1 us (5%)
  other arithmetic  27.9 us (4%)
  between operations  13.5 us (2%)
  starting transfers between devices  12 us (2%)
    scatter x1, local copies, waits for them, and re-layouts, per_device(): send_buffer = jnp.zeros((experts, capacity, model_width), jnp.bfloat16).a...  158 us
    all_to_all x1, blocking collectives, per_device(): lax.all_to_all(send_buffer, ('ctx', 'exp'), split_axis=0, concat_axis=0,...  127 us
    all_to_all x1, waiting for transfers between devices, per_device(): lax.all_to_all(finished, ('ctx', 'exp'), split_axis=0, concat_axis=0, til...  120 us
    all_gather x1, waiting for transfers between devices, per_device(): lax.all_gather(out_proj, 'ctx', axis=1, tiled=True)  74.2 us
    all_gather x1, waiting for transfers between devices, carried_in(): everything = jax.tree.map(lambda part: lax.all_gather(part, axis), array)  51.4 us
    dot_general x1, matrix products, per_device(): jnp.dot(inner, down_weight[0], preferred_element_type=jnp.float32)  18.8 us
    gather x1, local copies, waits for them, and re-layouts, per_device(): returned[flat_ids, slots].reshape(tok_rows, top_count, model_width)  16.7 us
  transfers between devices with their start and end apart: 6, of which 4 were waited for; matrix products, arithmetic and copies ran while one was open for 5% of the time, Pallas kernels for 0%

commit v1 on v0

--- a/solution.py
+++ b/solution.py
@@ -8,6 +8,18 @@
 KERNEL = 4
 EPS = 1e-05
 HIGH = lax.Precision.HIGHEST
+
+
+def gather_by_bits(x, axis, dim):
+    ways, here = (lax.axis_size(axis), lax.axis_index(axis))
+    grown, reach = (x, 1)
+    while reach < ways:
+        theirs = lax.ppermute(grown, axis, [(d, d ^ reach) for d in range(ways)])
+        mine_first = jnp.concatenate([grown, theirs], axis=dim)
+        theirs_first = jnp.concatenate([theirs, grown], axis=dim)
+        grown = jnp.where(here & reach == 0, mine_first, theirs_first)
+        reach = 2 * reach
+    return grown
 
 
 def from_behind(array, axis, by):
@@ -123,9 +135,7 @@
         .astype(jnp.bfloat16)
     )
     partial_out = jnp.dot(
-        normed,
-        lax.all_gather(out_proj, "ctx", axis=1, tiled=True),
-        preferred_element_type=jnp.float32,
+        normed, gather_by_bits(out_proj, "ctx", 1), preferred_element_type=jnp.float32
     )
     mixed = lax.psum_scatter(partial_out, "exp", scatter_dimension=0, tiled=True)
     hidden_f = (residual.astype(jnp.float32) + mixed).astype(jnp.bfloat16).astype(jnp.float32)

time: 688 us -> 759 us (1.10)
  blocking collectives: 137 us -> 196 us
    ppermute x0 -> x3, waiting for transfers between devices: none -> 126 us  [gather_by_bits(): theirs = lax.ppermute(grown, axis, [(d, d ^ reach) for d in range(ways)])]
    all_gather x1 -> x0, waiting for transfers between devices: 74.2 us -> none  [per_device(): lax.all_gather(out_proj, 'ctx', axis=1, tiled=True)]
    all_gather x1, blocking collectives: 10.8 us -> 69.5 us  [carried_in(): everything = jax.tree.map(lambda part: lax.all_gather(part, axis), array)]
    all_gather x1, waiting for transfers between devices: 51.4 us -> 0.01 us  [carried_in(): everything = jax.tree.map(lambda part: lax.all_gather(part, axis), array)]
  transfers between devices with their start and end apart: 6 -> 8, of which waited for: 4 -> 4; matrix products, arithmetic and copies ran while one was open for 5% -> 5% of each run, Pallas kernels for 0% -> 0%
where the time goes in v1:
time: 759 us; the launch traced here: 755 us
  waiting for transfers between devices  256 us (34%)
  local copies, waits for them, and re-layouts  202 us (27%)
  blocking collectives  196 us (26%)
  matrix products  36.1 us (5%)
  other arithmetic  34.1 us (4%)
  starting transfers between devices  16.5 us (2%)
  between operations  13.9 us (2%)
    scatter x1, local copies, waits for them, and re-layouts, per_device(): send_buffer = jnp.zeros((experts, capacity, model_width), jnp.bfloat16).a...  158 us
    all_to_all x1, blocking collectives, per_device(): lax.all_to_all(send_buffer, ('ctx', 'exp'), split_axis=0, concat_axis=0,...  127 us
    ppermute x3, waiting for transfers between devices, gather_by_bits(): theirs = lax.ppermute(grown, axis, [(d, d ^ reach) for d in range(ways)])  126 us
    all_to_all x1, waiting for transfers between devices, per_device(): lax.all_to_all(finished, ('ctx', 'exp'), split_axis=0, concat_axis=0, til...  120 us
    all_gather x1, blocking collectives, carried_in(): everything = jax.tree.map(lambda part: lax.all_gather(part, axis), array)  69.5 us
    dot_general x1, matrix products, per_device(): jnp.dot(inner, down_weight[0], preferred_element_type=jnp.float32)  18.8 us
    gather x1, local copies, waits for them, and re-layouts, per_device(): returned[flat_ids, slots].reshape(tok_rows, top_count, model_width)  16.7 us
  transfers between devices with their start and end apart: 8, of which 4 were waited for; matrix products, arithmetic and copies ran while one was open for 5% of the time, Pallas kernels for 0%

profile of v1, /device:TPU:13, one launch (start us, length us, event | category | flops | bytes accessed | tf_op | source)
XLA Modules:
  0.0 754.7 jit_solution(3795802522757058981)
XLA Ops:
  6.5 0.7 slice.88
  7.5 3.1 collective-permute-start.1
  10.6 0.7 slice.79
  11.4 3.1 collective-permute-start
  14.5 0.9 slice_convert_fusion.3
  15.4 1.2 reduce-window.14
  17.0 0.9 copy.94
  18.2 0.7 bitcast_convert_fusion.3
  18.9 1.1 copy.98
  20.4 0.8 multiply_convert_fusion.4
  21.4 0.6 multiply_convert_fusion.2
  22.2 1.5 fusion.36
  24.1 20.3 %collective-permute-done.2 = bf16[1024,336]{0,1:T(8,128)(2,1)} collective-permute-done((bf16[1024,336]{0,1:T(8,128)(2,1)S(1)}, bf16[1024,336]{0,1:T(8,128)(2,1)}, u32[]{:S(2)}, u32[]{:S(2)}) %collective-permute-start.2) | collective-permute-done | bytes 688160 | tf_op jit(solution)/shard_map/ppermute | solution.py:17
  44.4 2.4 maximum_select_fusion.3
  47.2 0.7 copy.101
  47.9 0.7 copy.93
  48.6 2.2 copy.107
  50.8 0.7 mul.308
  52.1 69.5 %all_gather.10 = f32[8,2,8]{2,1,0:T(2,128)S(1)} all-gather(f32[1,2,8]{2,1,0:T(2,128)S(1)} %get-tuple-element.171), channel_id=1, replica_groups=mesh['groups'=2,'ctx'=8,'exp'=2] {'ctx'}, dimensions={0}, use_global_device_ids=true | all-gather | bytes 576 | tf_op jit(solution)/shard_map/all_gather | solution.py:33
  122.1 5.2 fusion.30
  127.3 3.8 maximum_select_fusion.2
  131.0 3.8 collective-permute-start.4
  134.9 9.7 %while.16 = (s32[]{:T(128)}, f32[2,8]{1,0:T(2,128)S(1)}, f32[2,8,64,128]{3,2,1,0:T(8,128)S(1)}, s32[]{:T(128)}, f32[8,2,8]{2,1,0:T(2,128)S(1)}, /*index=5*/f32[8,2,8,64,128]{4,3,2,1,0:T(8,128)}, s32[]{:T(128)}, s32[]{:T(128)}) while((s32[]{:T(128)}, f32[2,8]{1,0:T(2,128)S(1)}, f32[2,8,64,128]{3,2,1,0:T(8,128)S(1)}, s32[]{:T(128)}, ...), condition=%wide.region_3.4_spmd.clone, body=%wide.region_2.3_spmd.clone.sunk | while | flops 524340 | bytes 1573299 | solution.py:45
  134.9 1.2 fusion.78
  136.1 1.2 fusion.78
  137.3 1.2 fusion.78
  138.5 1.2 fusion.78
  139.8 1.2 fusion.78
  141.0 1.2 fusion.78
  142.2 1.2 fusion.78
  143.4 1.2 fusion.78
  144.6 2.3 multiply_reduce_fusion.1
  148.0 105.3 %collective-permute-done.4 = bf16[1024,1344]{0,1:T(8,128)(2,1)} collective-permute-done((bf16[1024,1344]{0,1:T(8,128)(2,1)}, bf16[1024,1344]{0,1:T(8,128)(2,1)}, u32[]{:S(2)}, u32[]{:S(2)}) %collective-permute-start.4) | collective-permute-done | bytes 2752544 | tf_op jit(solution)/shard_map/ppermute | solution.py:17
  253.3 8.1 %fusion.1 = f32[256,2688]{1,0:T(8,128)} fusion(bf16[1024,1344]{0,1:T(8,128)(2,1)} %collective-permute-done.4, bf16[1024,1344]{0,1:T(8,128)(2,1)} %maximum_select_fusion.2, pred[]{:T(512)S(6)} %eq.34, f32[256,1024]{1,0:T(8,128)S(1)} %bitcast.126, f32[256,1024]{1,0:T(8,128)S(1)} %copy.106, f32[1024]{0:T(1024)S(1)} %copy-done.12, bf16[256,1024]{1,0:T(8,128)(2,1)} %param.21), kind=kOutput, calls=%fused_computation.10 | convolution fusion | flops 1436418048 | bytes 10883073 | tf_op jit(solution)/shard_map/dot_general | solution.py:137
  262.2 1.7 reduce-window.16
  264.4 10.0 %reduce-scatter.2.cloned.1.call-done = f32[128,2688]{1,0:T(8,128)} async-done(((f32[256,2688]{1,0:T(8,128)}), f32[128,2688]{1,0:T(8,128)}) %reduce-scatter.2.cloned.1.call-update) | async-done | bytes 1376272 | tf_op jit(solution)/shard_map/reduce_scatter | solution.py:140
  274.4 1.6 fusion.26
  276.3 4.9 gather_fusion
  281.1 3.0 broadcast_in_dim.27
  284.1 158.3 %scatter_fusion = bf16[16,64,2688]{2,1,0:T(8,128)(2,1)} fusion(bf16[16,64,2688]{2,1,0:T(8,128)(2,1)} %broadcast_in_dim.27, s32[768]{0:T(1024)S(1)} %get-tuple-element.151, bf16[768,2688]{1,0:T(8,128)(2,1)} %gather_fusion), kind=kCustom, calls=%fused_computation.2 | custom fusion | bytes 12392448 | tf_op jit(solution)/shard_map/scatter | solution.py:162
  442.4 126.7 %all_to_all.10 = bf16[16,64,2688]{2,1,0:T(8,128)(2,1)} all-to-all(bf16[16,64,2688]{2,1,0:T(8,128)(2,1)} %scatter_fusion), channel_id=1, replica_groups=mesh['groups'=2,'ctx'=8,'exp'=2] {'ctx','exp'}, dimensions={0} | all-to-all | bytes 11010048 | tf_op jit(solution)/shard_map/all_to_all | solution.py:164
  569.1 18.8 %convolution_convert_fusion = bf16[1024,2688]{1,0:T(8,128)(2,1)} fusion(bf16[1,928,2688]{2,1,0:T(8,128)(2,1)} %param.35, bf16[1024,2688]{1,0:T(8,128)(2,1)} %bitcast.115, bf16[1,2688,928]{1,2,0:T(8,128)(2,1)} %param.34), kind=kOutput, calls=%fused_computation.8 | convolution fusion | flops 10222927872 | bytes 20987904 | tf_op jit(solution)/shard_map/dot_general | solution.py:169
  587.9 5.6 all-to-all-start.1
  593.7 120.5 %all-to-all-done.1 = bf16[16,64,2688]{2,1,0:T(8,128)(2,1)} async-done(((bf16[16,64,2688]{2,1,0:T(8,128)(2,1)}), bf16[16,64,2688]{2,1,0:T(8,128)(2,1)}, u32[]{:S(2)}, u32[]{:S(2)}) %all-to-all-start.1) | async-done | bytes 5505056 | tf_op jit(solution)/shard_map/all_to_all | solution.py:173
  714.1 16.7 %gather_fusion.1 = bf16[768,2688]{1,0:T(8,128)(2,1)} fusion(bf16[16,64,2688]{2,1,0:T(8,128)(2,1)} %all-to-all-done.1, s32[768]{0:T(1024)S(1)} %get-tuple-element.150), kind=kCustom, calls=%fused_computation.1 | custom fusion | bytes 8263680 | tf_op jit(solution)/shard_map/gather | solution.py:174
  730.8 7.9 %reshape.218 = f32[128,6,2688]{2,1,0:T(8,128)} reshape(bf16[768,2688]{1,0:T(8,128)(2,1)} %gather_fusion.1) | data formatting | bytes 12386304 | tf_op jit(solution)/shard_map/convert_element_type | solution.py:175
  738.7 8.1 %multiply_reduce_fusion = f32[128,2688]{1,0:T(8,128)S(1)} fusion(f32[128,6,2688]{2,1,0:T(8,128)} %reshape.218, f32[128,6]{1,0:T(8,128)S(1)} %copy.109), kind=kLoop, calls=%fused_computation.7 | loop fusion | flops 3784704 | bytes 9636864 | tf_op jit(solution)/shard_map/reduce_sum | solution.py:175
  746.8 1.0 fusion.29
  (94 shorter events, 6.1 us)
Async XLA Ops:
  6.5 8.8 %copy-start = (f32[256,16]{0,1:T(8,128)S(1)}, f32[256,16]{0,1:T(8,128)}, u32[]{:S(2)}) copy-start(f32[256,16]{0,1:T(8,128)} %param.23) | copy-start | bytes 49156
  6.5 14.7 %copy-start.5 = (bf16[256,1024]{1,0:T(8,128)(2,1)S(1)}, bf16[256,1024]{1,0:T(8,128)(2,1)}, u32[]{:S(2)}) copy-start(bf16[256,1024]{1,0:T(8,128)(2,1)} %param.19) | copy-start | bytes 1572868
  6.5 128.3 %all-gather.3.cloned.1.call-start = ((), (), s32[]{:S(2)}) async-start(), calls=%async_computation.4 | async-start | bytes 4718592 | tf_op jit(solution)/shard_map/all_gather | solution.py:33
  7.5 12.7 %collective-permute-start.1 = (bf16[3,2,256]{0,2,1:T(8,128)(2,1)S(1)}, bf16[3,2,256]{0,2,1:T(8,128)(2,1)S(1)}, u32[]{:S(2)}, u32[]{:S(2)}) collective-permute-start(bf16[3,2,256]{0,2,1:T(8,128)(2,1)S(1)} %copy.97), channel_id=1, source_target_pairs={{0,2},{2,4},{4,6},{6,8},{8,10},{10,12},{12,14},{1,3},{3,5},{5,7},{... | collective-permute-start | bytes 9224 | tf_op jit(solution)/shard_map/ppermute | solution.py:28
  11.4 9.8 %collective-permute-start = (bf16[3,1024]{1,0:T(4,128)(2,1)S(1)}, bf16[3,1024]{1,0:T(4,128)(2,1)S(1)}, u32[]{:S(2)}, u32[]{:S(2)}) collective-permute-start(bf16[3,1024]{1,0:T(4,128)(2,1)S(1)} %slice.79), channel_id=1, source_target_pairs={{0,2},{2,4},{4,6},{6,8},{8,10},{10,12},{12,14},{1,3},{3,5},{5,7},{... | collective-permute-start | bytes 18440 | tf_op jit(solution)/shard_map/ppermute | solution.py:28
  21.2 100.4 %copy-start.6 = (bf16[256,1,256]{0,2,1:T(8,128)(2,1)}, bf16[256,1,256]{0,2,1:T(8,128)(2,1)S(1)}, u32[]{:S(2)}) copy-start(bf16[256,1,256]{0,2,1:T(8,128)(2,1)S(1)} %get-tuple-element.172) | copy-start | bytes 393220
  21.4 2.4 copy-start.3
  22.0 28.8 %copy-start.14 = (f32[16]{0:T(128)S(1)}, f32[16]{0:T(128)}, u32[]{:S(2)}) copy-start(f32[16]{0:T(128)} %param.26) | copy-start | bytes 196
  22.0 29.4 %copy-start.13 = (bf16[1024]{0:T(1024)(128)(2,1)S(1)}, bf16[1024]{0:T(1024)(128)(2,1)}, u32[]{:S(2)}) copy-start(bf16[1024]{0:T(1024)(128)(2,1)} %param.28) | copy-start | bytes 6148
  23.7 250.7 %reduce-scatter.2.cloned.1.call-start = ((), (), s32[]{:S(2)}) async-start(), calls=%async_computation.3 | async-start | bytes 4128768 | tf_op jit(solution)/shard_map/reduce_scatter | solution.py:140
  23.8 20.6 %collective-permute-start.2 = (bf16[1024,336]{0,1:T(8,128)(2,1)S(1)}, bf16[1024,336]{0,1:T(8,128)(2,1)}, u32[]{:S(2)}, u32[]{:S(2)}) collective-permute-start(bf16[1024,336]{0,1:T(8,128)(2,1)S(1)} %copy-done.3), channel_id=1, source_target_pairs={{0,2},{2,0},{4,6},{6,4},{8,10},{10,8},{12,14},{14,12},{1,3},{3,1},... | collective-permute-start | bytes 2064392 | tf_op jit(solution)/shard_map/ppermute | solution.py:17
  46.8 80.5 %collective-permute-start.3 = (bf16[1024,672]{0,1:T(8,128)(2,1)S(1)}, bf16[1024,672]{0,1:T(8,128)(2,1)}, u32[]{:S(2)}, u32[]{:S(2)}) collective-permute-start(bf16[1024,672]{0,1:T(8,128)(2,1)S(1)} %maximum_select_fusion.3), channel_id=1, source_target_pairs={{0,4},{2,6},{4,0},{6,2},{8,12},{10,14},{12,8},{14,10},{1,5},{3,7},... | collective-permute-start | bytes 4128776 | tf_op jit(solution)/shard_map/ppermute | solution.py:17
  131.0 13.6 %copy-start.2 = (f32[256,1024]{0,1:T(8,128)S(1)}, f32[256,1024]{0,1:T(8,128)}, u32[]{:S(2)}) copy-start(f32[256,1024]{0,1:T(8,128)} %copy.107) | copy-start | bytes 3145732
  131.0 13.6 %copy-start.7 = (bf16[256,1,256]{0,2,1:T(8,128)(2,1)S(1)}, bf16[256,1,256]{0,2,1:T(8,128)(2,1)}, u32[]{:S(2)}) copy-start(bf16[256,1,256]{0,2,1:T(8,128)(2,1)} %copy-done.6) | copy-start | bytes 393220
  131.0 13.6 %copy-start.8 = (f32[256,2,8]{0,2,1:T(8,128)S(1)}, f32[256,2,8]{0,2,1:T(8,128)}, u32[]{:S(2)}) copy-start(f32[256,2,8]{0,2,1:T(8,128)} %copy.93) | copy-start | bytes 49156
  131.0 13.6 %copy-start.15 = (f32[2,8]{1,0:T(2,128)S(1)}, f32[2,8]{1,0:T(2,128)}, u32[]{:S(2)}) copy-start(f32[2,8]{1,0:T(2,128)} %mul.308) | copy-start | bytes 196
  131.0 122.3 %collective-permute-start.4 = (bf16[1024,1344]{0,1:T(8,128)(2,1)}, bf16[1024,1344]{0,1:T(8,128)(2,1)}, u32[]{:S(2)}, u32[]{:S(2)}) collective-permute-start(bf16[1024,1344]{0,1:T(8,128)(2,1)} %maximum_select_fusion.2), channel_id=1, source_target_pairs={{0,8},{2,10},{4,12},{6,14},{8,0},{10,2},{12,4},{14,6},{1,9},{3,11}... | collective-permute-start | bytes 8257544 | tf_op jit(solution)/shard_map/ppermute | solution.py:17
  146.9 106.4 %copy-start.12 = (f32[1024]{0:T(1024)S(1)}, f32[1024]{0:T(1024)}, u32[]{:S(2)}) copy-start(f32[1024]{0:T(1024)} %convert_element_type.82) | copy-start | bytes 12292
  253.3 8.2 %copy-start.10 = (s32[128,6]{0,1:T(8,128)S(1)}, s32[128,6]{0,1:T(8,128)}, u32[]{:S(2)}) copy-start(s32[128,6]{0,1:T(8,128)} %param.32) | copy-start | bytes 9220
  253.3 8.7 %copy-start.9 = (bf16[2688]{0:T(1024)(128)(2,1)S(1)}, bf16[2688]{0:T(1024)(128)(2,1)}, u32[]{:S(2)}) copy-start(bf16[2688]{0:T(1024)(128)(2,1)} %param.31) | copy-start | bytes 16132
  253.3 21.1 %copy-start.4 = (bf16[128,2688]{1,0:T(8,128)(2,1)S(1)}, bf16[128,2688]{1,0:T(8,128)(2,1)}, u32[]{:S(2)}) copy-start(bf16[128,2688]{1,0:T(8,128)(2,1)} %param.30) | copy-start | bytes 2064388
  587.9 5.6 copy-start.11
  587.9 126.2 %all-to-all-start.1 = ((bf16[16,64,2688]{2,1,0:T(8,128)(2,1)}), bf16[16,64,2688]{2,1,0:T(8,128)(2,1)}, u32[]{:S(2)}, u32[]{:S(2)}) async-start(bf16[16,64,2688]{2,1,0:T(8,128)(2,1)} %bitcast.114), calls=%async_computation.2 | async-start | bytes 11010048 | tf_op jit(solution)/shard_map/all_to_all | solution.py:173
  738.7 9.1 %copy-start.1 = (f32[256,16]{0,1:T(8,128)S(1)}, f32[256,16]{0,1:T(8,128)}, u32[]{:S(2)}) copy-start(f32[256,16]{0,1:T(8,128)} %param.23) | copy-start | bytes 49156
Sparse Core Ops, SparseCore 0:
  23.8 94.2 all-gather.2
  261.6 12.7 reduce-scatter.1
